TPU v7x, 32 devices: a whole 2x2x4 slice. The times are simulated.
32 devices in a mesh: dp: 4 (over z), expert: 8 (over y, x, core).
Axes of the slice: x: 2, y: 2, z: 4, core: 2. Of those that a mesh axis runs over, the one named last changes fastest.
Arguments:
- queries: bfloat16 [8192, 1536], P(('dp', 'expert')), may hold values from -8 to 8
- rotated_key_heads: bfloat16 [8192, 512], P(('dp', 'expert')), may hold values from -8 to 8
- token_value_heads: bfloat16 [8192, 512], P(('dp', 'expert')), may hold values from -4 to 4
- residual: bfloat16 [8192, 1536], P(('dp', 'expert')), may hold values from -20 to 20
- lengths: int32 [32, 4], P(('dp', 'expert')), may hold values from 1 to 128, 256 in all within a row
- request_adapter_index: int32 [128], P(('dp', 'expert')), may hold values from 0 to 63
- attention_output_weight: bfloat16 [1536, 1536], P('dp'), may hold values from -0.15625 to 0.15625
- adapter_down_factor: bfloat16 [64, 1536, 16], P('expert'), may hold values from -0.15625 to 0.15625
- adapter_up_factor: bfloat16 [64, 16, 1536], P('expert'), may hold values from -1.5 to 1.5
- expert_norm_scale: float32 [1536], replicated, may hold values from 0.5 to 1.5
- router_logit_scores: float32 [8192, 8], P(('dp', 'expert')), may hold values from -4 to 404
- routes: int32 [8192, 8], P(('dp', 'expert')), may hold values from 0 to 15, all different within a row; in each aligned block of 256 rows (0 to 255, 256 to 511, ...) at most 160 rows name the same one
- expert_gate_weight: bfloat16 [16, 1536, 512], P('expert'), may hold values from -0.15625 to 0.15625
- expert_up_weight: bfloat16 [16, 1536, 512], P('expert'), may hold values from -0.15625 to 0.15625
- expert_down_weight: bfloat16 [16, 512, 1536], P('expert'), may hold values from -0.25 to 0.25
Outputs:
- block_out: bfloat16 [8192, 1536], P(('dp', 'expert'))
Inputs may be any that keep to these rules, and one draw needn't show every extreme that they name: `routes`: in the rows of one device no expert is named by more than 160 rows, a bound that some block reaches.
All inputs are finite; a program needn't handle non-finite values.
Results may differ from a plain program's by a relative error of at most 0.0044.
Values may be sent and summed in bfloat16 or wider, within the bound.
No kernel may reach another device: no remote copies, remote signals or barrier semaphores. Data moves between devices by JAX's collectives and lax.ppermute only.
A program may use at most 128 MiB of HBM per device.

v0:
```python
import jax
import jax.numpy as jnp
from jax import lax
from jax.sharding import PartitionSpec as P

HEADS = 24
KV_HEADS = 8
HEAD = 64
TOPK = 8


def segment_of(lengths_row, tokens):
    request_ends = jnp.cumsum(lengths_row)
    positions = jnp.arange(tokens, dtype=jnp.int32)
    return jnp.sum((positions[:, None] >= request_ends[None, :]).astype(jnp.int32), axis=1)


def attend(queries, rotated_key_heads, token_value_heads, segment):
    tokens = queries.shape[0]
    groups = HEADS // KV_HEADS
    grouped = queries.reshape(tokens, KV_HEADS, groups, HEAD)
    key_heads = rotated_key_heads.reshape(tokens, KV_HEADS, HEAD)
    value_heads = token_value_heads.reshape(tokens, KV_HEADS, HEAD)
    scores = jnp.einsum(
        "tkgh,skh->kgts", grouped, key_heads, preferred_element_type=jnp.float32
    ) * HEAD ** (-0.5)
    positions = jnp.arange(tokens, dtype=jnp.int32)
    allowed = (segment[:, None] == segment[None, :]) & (positions[:, None] >= positions[None, :])
    scores = jnp.where(allowed, scores, -1e30)
    row_peak = jnp.max(scores, axis=-1, keepdims=True)
    raised = jnp.exp(scores - row_peak)
    weights = (raised / jnp.sum(raised, axis=-1, keepdims=True)).astype(jnp.bfloat16)
    head_mix = jnp.einsum(
        "kgts,skh->tkgh", weights, value_heads, preferred_element_type=jnp.float32
    )
    return head_mix.reshape(tokens, HEADS * HEAD).astype(jnp.bfloat16)


def run_experts(arrived, expert_gate_weight, expert_up_weight, expert_down_weight):
    gate_part = jnp.einsum(
        "secd,edf->secf", arrived, expert_gate_weight, preferred_element_type=jnp.float32
    )
    up_part = jnp.einsum(
        "secd,edf->secf", arrived, expert_up_weight, preferred_element_type=jnp.float32
    )
    active = (jax.nn.silu(gate_part) * up_part).astype(jnp.bfloat16)
    return jnp.einsum(
        "secf,efd->secd", active, expert_down_weight, preferred_element_type=jnp.float32
    ).astype(jnp.bfloat16)


def per_device(
    queries,
    rotated_key_heads,
    token_value_heads,
    residual,
    lengths,
    request_adapter_index,
    attention_output_weight,
    adapter_down_factor,
    adapter_up_factor,
    expert_norm_scale,
    router_logit_scores,
    routes,
    expert_gate_weight,
    expert_up_weight,
    expert_down_weight,
):
    tokens = queries.shape[0]
    width = attention_output_weight.shape[1]
    requests_here = request_adapter_index.shape[0]
    segment = segment_of(lengths[0], tokens)
    context = attend(queries, rotated_key_heads, token_value_heads, segment)
    projected = jnp.dot(
        context,
        lax.all_gather(attention_output_weight, "dp", axis=0, tiled=True),
        preferred_element_type=jnp.float32,
    )
    member_int = (segment[:, None] == jnp.arange(requests_here, dtype=jnp.int32)[None, :]).astype(
        jnp.int32
    )
    pool_down, pool_up = (
        lax.all_gather(adapter_down_factor, "expert", axis=0, tiled=True),
        lax.all_gather(adapter_up_factor, "expert", axis=0, tiled=True),
    )
    chosen_down = jnp.take(pool_down, request_adapter_index, axis=0)
    chosen_up = jnp.take(pool_up, request_adapter_index, axis=0)
    rank_size = chosen_down.shape[2]
    every_low = jnp.einsum("td,rdk->trk", context, chosen_down, preferred_element_type=jnp.float32)
    picked_low = (every_low * member_int.astype(jnp.float32)[:, :, None]).astype(jnp.bfloat16)
    picked_low = picked_low.reshape(tokens, requests_here * rank_size)
    adapter_term = jnp.dot(
        picked_low,
        chosen_up.reshape(requests_here * rank_size, width),
        preferred_element_type=jnp.float32,
    )
    hidden = residual.astype(jnp.float32) + projected + adapter_term
    mean_square = jnp.mean(hidden * hidden, axis=-1, keepdims=True)
    normed = (hidden * lax.rsqrt(mean_square + 1e-06) * expert_norm_scale).astype(jnp.bfloat16)
    logit_peak = jnp.max(router_logit_scores, axis=-1, keepdims=True)
    raised = jnp.exp(router_logit_scores - logit_peak)
    gate_weights = raised / jnp.sum(raised, axis=-1, keepdims=True)
    local_experts = expert_gate_weight.shape[0]
    expert_devices = lax.axis_size("expert")
    experts_all = local_experts * expert_devices
    capacity = min(tokens, max(2, tokens * TOPK * 5 // (4 * experts_all)))
    flat_routes = routes.reshape(-1)
    route_hits = (flat_routes[:, None] == jnp.arange(experts_all, dtype=jnp.int32)[None, :]).astype(
        jnp.int32
    )
    slot_rank = jnp.sum((jnp.cumsum(route_hits, axis=0) - route_hits) * route_hits, axis=1)
    slot_index = flat_routes * capacity + slot_rank
    anchor = jnp.arange(tokens * TOPK, dtype=jnp.int32) // TOPK
    sources = jnp.zeros((experts_all * capacity,), jnp.int32).at[slot_index].set(anchor)
    filled = jnp.zeros((experts_all * capacity,), jnp.int32).at[slot_index].set(1)
    outgoing = jnp.where(
        filled[:, None] > 0, jnp.take(normed, sources, axis=0), jnp.zeros((), normed.dtype)
    )
    outgoing = outgoing.reshape(expert_devices, local_experts, capacity, width)
    arrived = lax.all_to_all(outgoing, "expert", split_axis=0, concat_axis=0, tiled=True)
    came_back = lax.all_to_all(
        run_experts(arrived, expert_gate_weight, expert_up_weight, expert_down_weight),
        "expert",
        split_axis=0,
        concat_axis=0,
        tiled=True,
    )
    picked = jnp.take(came_back.reshape(experts_all * capacity, width), slot_index, axis=0).reshape(
        tokens, TOPK, width
    )
    mixture = jnp.sum(gate_weights[:, :, None] * picked, axis=1)
    return (hidden + mixture).astype(jnp.bfloat16)


def solution(mesh):
    return jax.shard_map(
        per_device,
        mesh=mesh,
        in_specs=(
            P(("dp", "expert"), None),
            P(("dp", "expert"), None),
            P(("dp", "expert"), None),
            P(("dp", "expert"), None),
            P(("dp", "expert"), None),
            P(("dp", "expert")),
            P("dp", None),
            P("expert", None, None),
            P("expert", None, None),
            P(),
            P(("dp", "expert"), None),
            P(("dp", "expert"), None),
            P("expert", None, None),
            P("expert", None, None),
            P("expert", None, None),
        ),
        out_specs=P(("dp", "expert"), None),
        check_vma=False,
    )
```

profile of v0, /device:TPU:0, one launch (start us, length us, event | category | flops | bytes accessed | tf_op | source)
XLA Modules:
  0.0 456.1 jit_solution(2554271354359313261)
XLA Ops:
  6.5 0.0 copy-start
  6.5 0.7 all-gather.6.cloned.1.call-update
  7.3 0.0 all-gather.8.cloned.1.call-start
  7.3 0.7 all-gather.8.cloned.1.call-update
  8.0 0.0 all-gather.4.cloned.1.call-start
  8.1 0.7 all-gather.4.cloned.1.call-update
  8.7 0.8 copy.64
  9.6 0.1 eq.62
  9.7 0.1 reshape.168
  9.8 2.3 copy.59
  12.1 1.8 copy.58
  13.9 1.8 copy.60
  15.7 0.8 reduce-window.18
  16.5 4.5 reduce-window.19
  21.1 0.4 slice_reduce_fusion
  21.5 0.2 reduce-window.20
  21.7 0.1 copy.68
  21.8 0.1 mul.82
  22.0 0.1 broadcast_add_fusion
  22.1 0.1 fusion.34
  22.2 8.1 %scatter_custom_fusion.1 = s32[2560]{0:T(1024)S(1)} fusion(s32[2048]{0:T(1024)S(1)} %bitcast.120, s32[2048]{0:T(1024)S(1)} %add_select_fusion, s32[]{:T(128)} %constant.64.clone.1), kind=kCustom, calls=%fused_computation.74 | custom fusion | bytes 10244 | tf_op jit(solution)/shard_map/scatter | solution.py:114
  30.2 0.7 broadcast_in_dim.102
  30.9 8.1 %scatter_custom_fusion = s32[2560]{0:T(1024)S(1)} fusion(s32[2048]{0:T(1024)S(1)} %bitcast.121, s32[2048]{0:T(1024)S(1)} %broadcast.140, s32[]{:T(128)} %constant.64.clone.1), kind=kCustom, calls=%fused_computation.77 | custom fusion | bytes 10244 | tf_op jit(solution)/shard_map/scatter | solution.py:115
  39.0 0.7 broadcast_in_dim.100
  39.7 0.6 pad_clamp_fusion
  40.3 0.1 convert_reduce_fusion
  40.4 0.5 compare_and_fusion.2
  40.9 0.6 convert_convert_fusion
  41.5 0.1 fusion.29
  41.6 0.0 copy-start.5
  41.6 6.0 %fusion.51 = (f32[8,3,256]{2,1,0:T(4,128)S(1)}, f32[8,3,256,256]{2,3,1,0:T(8,128)}) fusion(pred[256,256]{0,1:T(8,128)(4,1)S(1)} %fusion.29, bf16[256,8,64,1]{0,2,3,1:T(8,128)(2,1)} %bitcast.117, bf16[256,8,3,64]{0,3,2,1:T(8,128)(2,1)} %bitcast.114), kind=kOutput, calls=%fused_computation.93 | convolution fusion | flops 207618304 | bytes 7430144 | tf_op jit(solution)/shard_map/sub | solution.py:31
  47.6 4.3 fusion.26
  52.0 0.0 copy-done.14
  52.0 2.6 gather_fusion
  54.6 24.0 %all-gather.8.cloned.1.call-done = bf16[64,16,1536]{2,1,0:T(8,128)(2,1)} async-done(((bf16[8,16,1536]{2,1,0:T(8,128)(2,1)}), bf16[64,16,1536]{2,1,0:T(8,128)(2,1)}) %all-gather.8.cloned.1.call-update) | async-done | bytes 3145744 | tf_op jit(solution)/shard_map/all_gather | solution.py:84
  78.6 2.6 gather_fusion.1
  81.2 0.7 broadcast_select_fusion
  81.8 1.4 fusion.52
  83.2 2.3 convolution_bitcast_fusion
  85.5 84.1 %all-gather.4.cloned.1.call-done = bf16[1536,1536]{1,0:T(8,128)(2,1)} async-done(((bf16[384,1536]{1,0:T(8,128)(2,1)}), bf16[1536,1536]{1,0:T(8,128)(2,1)}) %all-gather.4.cloned.1.call-update) | async-done | bytes 4718608 | tf_op jit(solution)/shard_map/all_gather | solution.py:76
  169.6 4.8 %multiply_reduce_fusion.1 = (f32[256]{0:T(256)S(1)}, f32[256,1536]{1,0:T(8,128)S(1)}) fusion(f32[256,1536]{1,0:T(8,128)} %convolution_bitcast_fusion, bf16[256,1536]{0,1:T(8,128)(2,1)} %bitcast.112, bf16[1536,1536]{1,0:T(8,128)(2,1)} %all-gather.4.cloned.1.call-done, bf16[256,1536]{1,0:T(8,128)(2,1)} %param.18), kind=kOutput, calls=%fused_computation.38 | convolution fusion | flops 1209925376 | bytes 9438208 | tf_op jit(solution)/shard_map/dot_general | solution.py:74
  174.4 0.0 copy-start.2
  174.4 1.2 copy-done.2
  175.6 1.1 multiply_convert_fusion
  176.6 17.6 %gather_fusion.2 = bf16[2560,1536]{1,0:T(8,128)(2,1)} fusion(bf16[256,1536]{1,0:T(8,128)(2,1)} %multiply_convert_fusion, s32[3072]{0:T(1024)S(1)} %copy-done.8), kind=kCustom, calls=%fused_computation.2 | custom fusion | bytes 15738880 | tf_op jit(solution)/shard_map/jit(_take)/gather | solution.py:117
  194.3 0.0 copy-done.10
  194.3 4.5 select_select_fusion
  198.7 0.0 copy-start.15
  198.7 92.1 %all_to_all.10 = bf16[8,2,160,1536]{3,2,1,0:T(8,128)(2,1)S(1)} all-to-all(bf16[8,2,160,1536]{3,2,1,0:T(8,128)(2,1)S(1)} %select_select_fusion), channel_id=1, replica_groups=mesh['dp'=4,'expert'=8] {'expert'}, dimensions={0} | all-to-all | bytes 15728640 | tf_op jit(solution)/shard_map/all_to_all | solution.py:120
  290.9 3.2 copy-done.4
  294.0 0.0 copy-done.15
  294.1 5.9 %fusion.1 = f32[2,8,160,512]{3,2,1,0:T(8,128)} fusion(bf16[8,2,160,1536]{3,2,1,0:T(8,128)(2,1)S(1)} %all_to_all.10, bf16[2,1536,512]{2,1,0:T(8,128)(2,1)S(1)} %copy-done.15), kind=kOutput, calls=%fused_computation.10 | convolution fusion | flops 4026531840 | bytes 16252928 | tf_op jit(solution)/shard_map/secd,edf->secf/dot_general | solution.py:43
  300.0 14.2 %convert_bitcast_fusion = bf16[8,2,160,1536]{3,2,0,1:T(8,128)(2,1)} fusion(bf16[2,512,1536]{2,1,0:T(8,128)(2,1)S(1)} %copy-done, f32[2,8,160,512]{3,2,1,0:T(8,128)} %fusion.1, bf16[2,1536,512]{2,1,0:T(8,128)(2,1)} %param.27, bf16[8,2,160,1536]{3,2,1,0:T(8,128)(2,1)} %copy-done.4), kind=kOutput, calls=%fused_computation.8 | convolution fusion | flops 8064860160 | bytes 27262976 | tf_op jit(solution)/shard_map/secf,efd->secd/dot_general | solution.py:47
  314.2 7.1 %copy.71 = bf16[8,2,160,1536]{3,2,1,0:T(8,128)(2,1)} copy(bf16[8,2,160,1536]{3,2,0,1:T(8,128)(2,1)} %convert_bitcast_fusion) | data formatting | bytes 15728640 | tf_op jit(solution)/shard_map/convert_element_type | solution.py:49
  321.3 5.0 %all-to-all-start.1 = ((bf16[8,2,160,1536]{3,2,1,0:T(8,128)(2,1)}), bf16[8,2,160,1536]{3,2,1,0:T(8,128)(2,1)}, u32[]{:S(2)}, u32[]{:S(2)}) async-start(bf16[8,2,160,1536]{3,2,1,0:T(8,128)(2,1)} %copy.71), calls=%async_computation.1 | async-start | bytes 15728640 | tf_op jit(solution)/shard_map/all_to_all | solution.py:121
  326.3 0.1 reduce_sum.62
  326.4 0.1 copy.66
  326.5 0.2 copy.67
  326.7 0.0 copy-done.7
  326.8 0.1 copy.63
  326.9 87.9 %all-to-all-done.1 = bf16[8,2,160,1536]{3,2,1,0:T(8,128)(2,1)} async-done(((bf16[8,2,160,1536]{3,2,1,0:T(8,128)(2,1)}), bf16[8,2,160,1536]{3,2,1,0:T(8,128)(2,1)}, u32[]{:S(2)}, u32[]{:S(2)}) %all-to-all-start.1) | async-done | bytes 7864352 | tf_op jit(solution)/shard_map/all_to_all | solution.py:121
  414.8 17.7 %gather_fusion.3 = bf16[2048,1536]{1,0:T(8,128)(2,1)} fusion(bf16[2560,1536]{1,0:T(8,128)(2,1)} %bitcast.30, s32[2048]{0:T(1024)S(1)} %broadcast_clamp_fusion), kind=kCustom, calls=%fused_computation.3 | custom fusion | bytes 12591104 | tf_op jit(solution)/shard_map/jit(_take)/gather | solution.py:128
  432.5 16.0 %multiply_reduce_fusion = f32[256,1536]{1,0:T(8,128)S(1)} fusion(bf16[2048,1536]{1,0:T(8,128)(2,1)} %gather_fusion.3, f32[256,8]{1,0:T(8,128)S(1)} %copy.63, pred[256,8]{1,0:T(8,128)(4,1)S(1)} %copy.67), kind=kLoop, calls=%fused_computation.7 | loop fusion | flops 12189696 | bytes 7874560 | tf_op jit(solution)/shard_map/reduce_sum | solution.py:131
  448.5 1.1 add_convert_fusion
  (42 shorter events, 0.2 us)
Async XLA Ops:
  6.5 293.4 %copy-start = (bf16[2,512,1536]{2,1,0:T(8,128)(2,1)S(1)}, bf16[2,512,1536]{2,1,0:T(8,128)(2,1)}, u32[]{:S(2)}) copy-start(bf16[2,512,1536]{2,1,0:T(8,128)(2,1)} %param.29) | copy-start | bytes 9437188
  6.5 15.1 %copy-start.6 = (s32[256,8]{0,1:T(8,128)S(1)}, s32[256,8]{0,1:T(8,128)}, u32[]{:S(2)}) copy-start(s32[256,8]{0,1:T(8,128)} %param.26) | copy-start | bytes 24580
  6.5 33.1 %copy-start.16 = (s32[4]{0:T(128)S(1)}, s32[4]{0:T(128)}, u32[]{:S(2)}) copy-start(s32[4]{0:T(128)} %param.20) | copy-start | bytes 52
  6.5 45.4 %all-gather.6.cloned.1.call-start = ((), (), s32[]{:S(2)}) async-start(), calls=%async_computation.3 | async-start | bytes 3538944 | tf_op jit(solution)/shard_map/all_gather | solution.py:83
  7.3 71.3 %all-gather.8.cloned.1.call-start = ((), (), s32[]{:S(2)}) async-start(), calls=%async_computation.4 | async-start | bytes 3538944 | tf_op jit(solution)/shard_map/all_gather | solution.py:84
  8.0 161.6 %all-gather.4.cloned.1.call-start = ((), (), s32[]{:S(2)}) async-start(), calls=%async_computation.2 | async-start | bytes 5898240 | tf_op jit(solution)/shard_map/all_gather | solution.py:76
  22.2 18.8 %copy-start.11 = (s32[2048,1]{0,1:T(1,128)}, s32[2048,1]{0,1:T(1,128)S(1)}, u32[]{:S(2)}) copy-start(s32[2048,1]{0,1:T(1,128)S(1)} %compare_select_fusion) | copy-start | bytes 24580
  39.7 12.3 %copy-start.14 = (s32[1024]{0:T(1024)}, s32[1024]{0:T(1024)S(1)}, u32[]{:S(2)}) copy-start(s32[1024]{0:T(1024)S(1)} %pad_clamp_fusion.1) | copy-start | bytes 12292
  41.6 6.0 %copy-start.5 = (bf16[256,512]{0,1:T(8,128)(2,1)S(1)}, bf16[256,512]{0,1:T(8,128)(2,1)}, u32[]{:S(2)}) copy-start(bf16[256,512]{0,1:T(8,128)(2,1)} %copy.60) | copy-start | bytes 786436
  85.5 90.1 %copy-start.13 = (f32[1536]{0:T(1024)S(1)}, f32[1536]{0:T(1024)}, u32[]{:S(2)}) copy-start(f32[1536]{0:T(1024)} %param.24) | copy-start | bytes 18436
  85.5 91.1 %copy-start.8 = (s32[3072]{0:T(1024)S(1)}, s32[3072]{0:T(1024)}, u32[]{:S(2)}) copy-start(s32[3072]{0:T(1024)} %pad_clamp_fusion) | copy-start | bytes 36868
  174.4 1.2 copy-start.2
  176.6 17.6 %copy-start.9 = (pred[8,2,160]{2,1,0:T(4,128)(4,1)S(1)}, pred[8,2,160]{2,1,0:T(4,128)(4,1)}, u32[]{:S(2)}) copy-start(pred[8,2,160]{2,1,0:T(4,128)(4,1)} %broadcast_in_dim.102) | copy-start | bytes 7684
  176.6 17.6 %copy-start.10 = (pred[8,2,160]{2,1,0:T(4,128)(4,1)S(1)}, pred[8,2,160]{2,1,0:T(4,128)(4,1)}, u32[]{:S(2)}) copy-start(pred[8,2,160]{2,1,0:T(4,128)(4,1)} %broadcast_in_dim.100) | copy-start | bytes 7684
  198.7 95.3 %copy-start.15 = (bf16[2,1536,512]{2,1,0:T(8,128)(2,1)S(1)}, bf16[2,1536,512]{2,1,0:T(8,128)(2,1)}, u32[]{:S(2)}) copy-start(bf16[2,1536,512]{2,1,0:T(8,128)(2,1)} %param.28) | copy-start | bytes 9437188
  290.9 3.2 copy-start.4
  321.3 5.4 %copy-start.7 = (f32[256,8]{0,1:T(8,128)S(1)}, f32[256,8]{0,1:T(8,128)}, u32[]{:S(2)}) copy-start(f32[256,8]{0,1:T(8,128)} %param.25) | copy-start | bytes 24580
  321.3 5.6 %copy-start.12 = (s32[2048,1]{0,1:T(1,128)S(1)}, s32[2048,1]{0,1:T(1,128)}, u32[]{:S(2)}) copy-start(s32[2048,1]{0,1:T(1,128)} %copy-done.11) | copy-start | bytes 24580
  321.3 93.5 %all-to-all-start.1 = ((bf16[8,2,160,1536]{3,2,1,0:T(8,128)(2,1)}), bf16[8,2,160,1536]{3,2,1,0:T(8,128)(2,1)}, u32[]{:S(2)}, u32[]{:S(2)}) async-start(bf16[8,2,160,1536]{3,2,1,0:T(8,128)(2,1)} %copy.71), calls=%async_computation.1 | async-start | bytes 15728640 | tf_op jit(solution)/shard_map/all_to_all | solution.py:121
  414.8 34.8 %copy-start.1 = (bf16[2,512,1536]{2,1,0:T(8,128)(2,1)S(1)}, bf16[2,512,1536]{2,1,0:T(8,128)(2,1)}, u32[]{:S(2)}) copy-start(bf16[2,512,1536]{2,1,0:T(8,128)(2,1)} %param.29) | copy-start | bytes 9437188
  432.5 16.0 %copy-start.3 = (f32[256,1536]{1,0:T(8,128)S(1)}, f32[256,1536]{1,0:T(8,128)}, u32[]{:S(2)}) copy-start(f32[256,1536]{1,0:T(8,128)} %copy-done.2) | copy-start | bytes 4718596
Sparse Core Ops, SparseCore 0:
  9.2 35.0 all-gather.5
  46.2 32.3 all-gather.7
  80.2 89.4 all-gather.3
where the time goes:
time: 457 us; the launch traced here: 456 us
  waiting for transfers between devices  198 us (43%)
  blocking collectives  92.1 us (20%)
  local copies, waits for them, and re-layouts  77.5 us (17%)
  matrix products  38.9 us (9%)
  other arithmetic  31 us (7%)
  between operations  13.4 us (3%)
  starting transfers between devices  5.11 us (1%)
    all_to_all x1, blocking collectives, per_device(): lax.all_to_all(outgoing, 'expert', split_axis=0, concat_axis=0, tiled=True)  92.1 us
    all_to_all x1, waiting for transfers between devices, per_device(): lax.all_to_all(run_experts(arrived, expert_gate_weight, expert_up_weight,...  87.9 us
    all_gather x1, waiting for transfers between devices, per_device(): lax.all_gather(attention_output_weight, 'dp', axis=0, tiled=True)  84.1 us
    all_gather x1, waiting for transfers between devices, per_device(): lax.all_gather(adapter_up_factor, 'expert', axis=0, tiled=True)  24 us
    gather x1, local copies, waits for them, and re-layouts, per_device(): jnp.take(came_back.reshape(experts_all * capacity, width), slot_index, ax...  17.7 us
    gather x1, local copies, waits for them, and re-layouts, per_device(): jnp.take(normed, sources, axis=0)  17.6 us
    reduce_sum x1, other arithmetic, per_device(): mixture = jnp.sum(gate_weights[:, :, None] * picked, axis=1)  16 us
    dot_general x1, matrix products, run_experts(): jnp.einsum('secf,efd->secd', active, expert_down_weight, preferred_elemen...  14.2 us
  transfers between devices with their start and end apart: 4, of which 3 were waited for; matrix products, arithmetic and copies ran while one was open for 12% of the time, Pallas kernels for 0%

commit v1 on v0

--- a/solution.py
+++ b/solution.py
@@ -7,6 +7,18 @@
 KV_HEADS = 8
 HEAD = 64
 TOPK = 8
+
+
+def split_up(x, dim, peers):
+    shape = x.shape
+    tiles = x.reshape(*shape[:dim], peers, shape[dim] // peers, *shape[dim + 1 :])
+    return jnp.moveaxis(tiles, dim, 0)
+
+
+def joined_along(blocks, dim):
+    blocks = jnp.moveaxis(blocks, 0, dim)
+    dims = blocks.shape
+    return blocks.reshape(*dims[:dim], dims[dim] * dims[dim + 1], *dims[dim + 2 :])
 
 
 def segment_of(lengths_row, tokens):
@@ -117,7 +129,14 @@
         filled[:, None] > 0, jnp.take(normed, sources, axis=0), jnp.zeros((), normed.dtype)
     )
     outgoing = outgoing.reshape(expert_devices, local_experts, capacity, width)
-    arrived = lax.all_to_all(outgoing, "expert", split_axis=0, concat_axis=0, tiled=True)
+    size, index = (lax.axis_size("expert"), lax.axis_index("expert"))
+    pieces = split_up(outgoing, 0, size)
+    outs = [pieces[index]]
+    for step in range(1, size):
+        sent = pieces[index ^ step]
+        outs.append(lax.ppermute(sent, "expert", [(i, i ^ step) for i in range(size)]))
+    pieces = jnp.stack(outs)[index ^ jnp.arange(size)]
+    arrived = joined_along(pieces, 0)
     came_back = lax.all_to_all(
         run_experts(arrived, expert_gate_weight, expert_up_weight, expert_down_weight),
         "expert",

time: 457 us -> 467 us (1.022)
  blocking collectives: 92.1 us -> 0 us
  waiting for transfers between devices: 198 us -> 270 us
  local copies, waits for them, and re-layouts: 77.5 us -> 91.1 us
  starting transfers between devices: 5.11 us -> 12.7 us
  other arithmetic: 31 us -> 36 us
  matrix products: 38.9 us -> 43.7 us
    all_to_all x1 -> x0, blocking collectives: 92.1 us -> none  [per_device(): lax.all_to_all(outgoing, 'expert', split_axis=0, concat_axis=0, tiled=True)]
    ppermute x0 -> x7, waiting for transfers between devices: none -> 77 us  [per_device(): lax.ppermute(sent, 'expert', [(i, i ^ step) for i in range(size)])]
    gather x0 -> x1, local copies, waits for them, and re-layouts: none -> 7.72 us  [per_device(): pieces = jnp.stack(outs)[index ^ jnp.arange(size)]]
    ppermute x0 -> x7, starting transfers between devices: none -> 7.34 us  [per_device(): lax.ppermute(sent, 'expert', [(i, i ^ step) for i in range(size)])]
    all_gather x1, waiting for transfers between devices: 24 us -> 18.7 us  [per_device(): lax.all_gather(adapter_up_factor, 'expert', axis=0, tiled=True)]
    dot_general x1, matrix products: 5.91 us -> 10.7 us  [run_experts(): jnp.einsum('secd,edf->secf', arrived, expert_gate_weight, preferred_eleme...]
    unnamed x38 -> x32, local copies, waits for them, and re-layouts: 11.1 us -> 14.1 us
  transfers between devices with their start and end apart: 4 -> 11, of which waited for: 3 -> 6; matrix products, arithmetic and copies ran while one was open for 12% -> 14% of each run, Pallas kernels for 0% -> 0%
where the time goes in v1:
time: 467 us; the launch traced here: 466 us
  waiting for transfers between devices  270 us (58%)
  local copies, waits for them, and re-layouts  91.1 us (20%)
  matrix products  43.7 us (9%)
  other arithmetic  36 us (8%)
  between operations  13.4 us (3%)
  starting transfers between devices  12.7 us (3%)
    all_to_all x1, waiting for transfers between devices, per_device(): lax.all_to_all(run_experts(arrived, expert_gate_weight, expert_up_weight,...  87.8 us
    all_gather x1, waiting for transfers between devices, per_device(): lax.all_gather(attention_output_weight, 'dp', axis=0, tiled=True)  84.1 us
    ppermute x7, waiting for transfers between devices, per_device(): lax.ppermute(sent, 'expert', [(i, i ^ step) for i in range(size)])  77 us
    all_gather x1, waiting for transfers between devices, per_device(): lax.all_gather(adapter_up_factor, 'expert', axis=0, tiled=True)  18.7 us
    gather x1, local copies, waits for them, and re-layouts, per_device(): jnp.take(normed, sources, axis=0)  17.9 us
    gather x1, local copies, waits for them, and re-layouts, per_device(): jnp.take(came_back.reshape(experts_all * capacity, width), slot_index, ax...  17.5 us
    reduce_sum x1, other arithmetic, per_device(): mixture = jnp.sum(gate_weights[:, :, None] * picked, axis=1)  16 us
    dot_general x1, matrix products, run_experts(): jnp.einsum('secf,efd->secd', active, expert_down_weight, preferred_elemen...  14.1 us
  transfers between devices with their start and end apart: 11, of which 6 were waited for; matrix products, arithmetic and copies ran while one was open for 14% of the time, Pallas kernels for 0%

profile of v1, /device:TPU:0, one launch (start us, length us, event | category | flops | bytes accessed | tf_op | source)
XLA Modules:
  0.0 466.5 jit_solution(15705039294598872378)
XLA Ops:
  6.5 0.7 all-gather.6.cloned.1.call-update
  7.3 0.7 all-gather.8.cloned.1.call-update
  8.1 0.7 all-gather.4.cloned.1.call-update
  8.7 0.8 copy.62
  9.8 1.3 reduce-window.18
  11.2 2.3 copy.57
  13.5 1.8 copy.56
  15.2 1.8 copy.58
  17.1 4.5 reduce-window.19
  21.6 0.4 slice_reduce_fusion
  22.0 0.2 reduce-window.20
  22.2 0.7 broadcast_multiply_fusion
  23.1 0.7 mul.82
  23.8 0.6 add_select_fusion
  24.5 0.7 compare_select_fusion
  25.3 8.2 %scatter_custom_fusion.1 = s32[2560]{0:T(1024)S(1)} fusion(s32[2048]{0:T(1024)S(1)} %bitcast.151, s32[2048]{0:T(1024)} %add_select_fusion, s32[]{:T(128)} %constant.58.clone.1), kind=kCustom, calls=%fused_computation.90 | custom fusion | bytes 10752 | tf_op jit(solution)/shard_map/scatter | solution.py:126
  33.6 8.1 %scatter_custom_fusion = s32[2560]{0:T(1024)S(1)} fusion(s32[2048]{0:T(1024)S(1)} %bitcast.152, s32[2048]{0:T(1024)S(1)} %broadcast.195, s32[]{:T(128)} %constant.58.clone.1), kind=kCustom, calls=%fused_computation.93 | custom fusion | bytes 10244 | tf_op jit(solution)/shard_map/scatter | solution.py:127
  41.7 0.7 broadcast_in_dim.101
  42.4 0.7 compare_select_fusion.4
  43.0 0.6 pad_clamp_fusion.2
  43.6 0.6 pad_clamp_fusion
  44.2 0.7 convert_reduce_fusion
  44.9 1.1 compare_and_fusion.2
  46.1 0.6 convert_convert_fusion
  46.8 5.9 %fusion.52 = (f32[8,3,256]{2,1,0:T(4,128)S(1)}, f32[8,3,256,256]{2,3,1,0:T(8,128)}) fusion(pred[256,256]{0,1:T(8,128)(4,1)S(1)} %fusion.29, bf16[256,8,64,1]{0,2,3,1:T(8,128)(2,1)} %bitcast.148, bf16[256,8,3,64]{0,3,2,1:T(8,128)(2,1)} %bitcast.145), kind=kOutput, calls=%fused_computation.112 | convolution fusion | flops 207618304 | bytes 7430144 | tf_op jit(solution)/shard_map/sub | solution.py:43
  52.7 4.6 fusion.26
  57.3 2.6 gather_fusion
  59.9 18.7 %all-gather.8.cloned.1.call-done = bf16[64,16,1536]{2,1,0:T(8,128)(2,1)} async-done(((bf16[8,16,1536]{2,1,0:T(8,128)(2,1)}), bf16[64,16,1536]{2,1,0:T(8,128)(2,1)}) %all-gather.8.cloned.1.call-update) | async-done | bytes 3145744 | tf_op jit(solution)/shard_map/all_gather | solution.py:96
  78.5 2.6 gather_fusion.1
  81.1 0.7 broadcast_select_fusion
  81.8 1.4 fusion.53
  83.2 2.3 convolution_bitcast_fusion
  85.5 84.1 %all-gather.4.cloned.1.call-done = bf16[1536,1536]{1,0:T(8,128)(2,1)} async-done(((bf16[384,1536]{1,0:T(8,128)(2,1)}), bf16[1536,1536]{1,0:T(8,128)(2,1)}) %all-gather.4.cloned.1.call-update) | async-done | bytes 4718608 | tf_op jit(solution)/shard_map/all_gather | solution.py:88
  169.6 4.8 %multiply_reduce_fusion.1 = (f32[256]{0:T(256)S(1)}, f32[256,1536]{1,0:T(8,128)S(1)}) fusion(f32[256,1536]{1,0:T(8,128)} %convolution_bitcast_fusion, bf16[256,1536]{0,1:T(8,128)(2,1)} %bitcast.143, bf16[1536,1536]{1,0:T(8,128)(2,1)} %all-gather.4.cloned.1.call-done, bf16[256,1536]{1,0:T(8,128)(2,1)} %param.18), kind=kOutput, calls=%fused_computation.39 | convolution fusion | flops 1209925376 | bytes 9438208 | tf_op jit(solution)/shard_map/dot_general | solution.py:86
  174.4 1.1 copy-done.1
  175.5 1.1 multiply_convert_fusion
  176.6 17.9 %gather_fusion.2 = bf16[2560,1536]{1,0:T(8,128)(2,1)} fusion(bf16[256,1536]{1,0:T(8,128)(2,1)} %multiply_convert_fusion, s32[3072]{0:T(1024)S(1)} %copy-done.6), kind=kCustom, calls=%fused_computation.2 | custom fusion | bytes 15738880 | tf_op jit(solution)/shard_map/jit(_take)/gather | solution.py:129
  194.5 4.5 select_select_fusion
  198.9 1.7 dynamic-slice_bitcast_fusion
  200.6 1.5 collective-permute-start.1
  202.1 0.4 collective-permute-start.2
  202.5 1.5 collective-permute-start.3
  204.2 2.4 collective-permute-start.5
  206.6 1.0 bitcast_dynamic-update-slice_fusion.6
  207.6 17.5 %collective-permute-done.1 = bf16[1,2,160,1536]{3,2,1,0:T(8,128)(2,1)S(1)} collective-permute-done((bf16[1,2,160,1536]{3,2,1,0:T(8,128)(2,1)S(1)}, bf16[1,2,160,1536]{3,2,1,0:T(8,128)(2,1)S(1)}, u32[]{:S(2)}, u32[]{:S(2)}) %collective-permute-start.1) | collective-permute-done | bytes 983072 | tf_op jit(solution)/shard_map/ppermute | solution.py:137
  225.1 1.4 collective-permute-start.6
  226.5 1.0 bitcast_dynamic-update-slice_fusion.5
  227.5 17.9 %collective-permute-done.2 = bf16[1,2,160,1536]{3,2,1,0:T(8,128)(2,1)S(1)} collective-permute-done((bf16[1,2,160,1536]{3,2,1,0:T(8,128)(2,1)S(1)}, bf16[1,2,160,1536]{3,2,1,0:T(8,128)(2,1)S(1)}, u32[]{:S(2)}, u32[]{:S(2)}) %collective-permute-start.2) | collective-permute-done | bytes 983072 | tf_op jit(solution)/shard_map/ppermute | solution.py:137
  245.4 1.0 bitcast_dynamic-update-slice_fusion.4
  246.5 1.0 bitcast_dynamic-update-slice_fusion.3
  247.5 41.5 %collective-permute-done.4 = bf16[1,2,160,1536]{3,2,1,0:T(8,128)(2,1)S(1)} collective-permute-done((bf16[1,2,160,1536]{3,2,1,0:T(8,128)(2,1)S(1)}, bf16[1,2,160,1536]{3,2,1,0:T(8,128)(2,1)S(1)}, u32[]{:S(2)}, u32[]{:S(2)}) %collective-permute-start.4) | collective-permute-done | bytes 983072 | tf_op jit(solution)/shard_map/ppermute | solution.py:137
  289.0 1.0 bitcast_dynamic-update-slice_fusion.2
  290.1 1.0 bitcast_dynamic-update-slice_fusion.1
  291.1 1.1 bitcast_dynamic-update-slice_fusion
  292.2 7.7 %gather_fusion.3 = bf16[8,2,160,1536]{3,2,1,0:T(8,128)(2,1)} fusion(bf16[8,2,160,1536]{3,2,1,0:T(8,128)(2,1)} %bitcast.35, s32[1024]{0:T(1024)S(1)} %pad_clamp_fusion.1), kind=kCustom, calls=%fused_computation.3 | custom fusion | bytes 15728672 | tf_op jit(solution)/shard_map/gather | solution.py:138
  299.9 10.7 %fusion.3 = f32[2,8,160,512]{3,2,1,0:T(8,128)} fusion(bf16[8,2,160,1536]{3,2,1,0:T(8,128)(2,1)} %gather_fusion.3, bf16[2,1536,512]{2,1,0:T(8,128)(2,1)} %param.27), kind=kOutput, calls=%fused_computation.13 | convolution fusion | flops 4026531840 | bytes 16252928 | tf_op jit(solution)/shard_map/secd,edf->secf/dot_general | solution.py:52
  310.6 14.1 %convert_bitcast_fusion = bf16[8,2,160,1536]{3,2,0,1:T(8,128)(2,1)} fusion(bf16[2,512,1536]{2,1,0:T(8,128)(2,1)S(1)} %copy-done, f32[2,8,160,512]{3,2,1,0:T(8,128)} %fusion.3, bf16[2,1536,512]{2,1,0:T(8,128)(2,1)} %param.28, bf16[8,2,160,1536]{3,2,1,0:T(8,128)(2,1)} %gather_fusion.3), kind=kOutput, calls=%fused_computation.9 | convolution fusion | flops 8064860160 | bytes 27262976 | tf_op jit(solution)/shard_map/secf,efd->secd/dot_general | solution.py:59
  324.7 7.0 %copy.69 = bf16[8,2,160,1536]{3,2,1,0:T(8,128)(2,1)} copy(bf16[8,2,160,1536]{3,2,0,1:T(8,128)(2,1)} %convert_bitcast_fusion) | data formatting | bytes 15728640 | tf_op jit(solution)/shard_map/convert_element_type | solution.py:61
  331.7 5.2 %all-to-all-start = ((bf16[8,2,160,1536]{3,2,1,0:T(8,128)(2,1)}), bf16[8,2,160,1536]{3,2,1,0:T(8,128)(2,1)}, u32[]{:S(2)}, u32[]{:S(2)}) async-start(bf16[8,2,160,1536]{3,2,1,0:T(8,128)(2,1)} %copy.69), calls=%async_computation | async-start | bytes 15728640 | tf_op jit(solution)/shard_map/all_to_all | solution.py:140
  337.1 0.2 copy.65
  337.5 87.8 %all-to-all-done = bf16[8,2,160,1536]{3,2,1,0:T(8,128)(2,1)} async-done(((bf16[8,2,160,1536]{3,2,1,0:T(8,128)(2,1)}), bf16[8,2,160,1536]{3,2,1,0:T(8,128)(2,1)}, u32[]{:S(2)}, u32[]{:S(2)}) %all-to-all-start) | async-done | bytes 7864352 | tf_op jit(solution)/shard_map/all_to_all | solution.py:140
  425.3 17.5 %gather_fusion.4 = bf16[2048,1536]{1,0:T(8,128)(2,1)} fusion(bf16[2560,1536]{1,0:T(8,128)(2,1)} %bitcast.46, s32[2048]{0:T(1024)S(1)} %broadcast_clamp_fusion), kind=kCustom, calls=%fused_computation.4 | custom fusion | bytes 12591104 | tf_op jit(solution)/shard_map/jit(_take)/gather | solution.py:147
  442.9 16.0 %multiply_reduce_fusion = f32[256,1536]{1,0:T(8,128)S(1)} fusion(bf16[2048,1536]{1,0:T(8,128)(2,1)} %gather_fusion.4, f32[256,8]{1,0:T(8,128)S(1)} %copy.61, pred[256,8]{1,0:T(8,128)(4,1)S(1)} %copy.65), kind=kLoop, calls=%fused_computation.8 | loop fusion | flops 12189696 | bytes 7874560 | tf_op jit(solution)/shard_map/reduce_sum | solution.py:150
  458.9 1.1 add_convert_fusion
  (54 shorter events, 1.3 us)
Async XLA Ops:
  6.5 304.1 %copy-start = (bf16[2,512,1536]{2,1,0:T(8,128)(2,1)S(1)}, bf16[2,512,1536]{2,1,0:T(8,128)(2,1)}, u32[]{:S(2)}) copy-start(bf16[2,512,1536]{2,1,0:T(8,128)(2,1)} %param.29) | copy-start | bytes 9437188
  6.5 50.7 %all-gather.6.cloned.1.call-start = ((), (), s32[]{:S(2)}) async-start(), calls=%async_computation.2 | async-start | bytes 3538944 | tf_op jit(solution)/shard_map/all_gather | solution.py:95
  7.3 71.3 %all-gather.8.cloned.1.call-start = ((), (), s32[]{:S(2)}) async-start(), calls=%async_computation.3 | async-start | bytes 3538944 | tf_op jit(solution)/shard_map/all_gather | solution.py:96
  8.0 161.6 %all-gather.4.cloned.1.call-start = ((), (), s32[]{:S(2)}) async-start(), calls=%async_computation.1 | async-start | bytes 5898240 | tf_op jit(solution)/shard_map/all_gather | solution.py:88
  23.8 28.9 %copy-start.3 = (bf16[256,512]{0,1:T(8,128)(2,1)S(1)}, bf16[256,512]{0,1:T(8,128)(2,1)}, u32[]{:S(2)}) copy-start(bf16[256,512]{0,1:T(8,128)(2,1)} %copy.58) | copy-start | bytes 786436
  25.3 20.8 %copy-start.8 = (s32[2048,1]{0,1:T(1,128)}, s32[2048,1]{0,1:T(1,128)S(1)}, u32[]{:S(2)}) copy-start(s32[2048,1]{0,1:T(1,128)S(1)} %compare_select_fusion) | copy-start | bytes 24580
  85.5 90.1 %copy-start.10 = (f32[1536]{0:T(1024)S(1)}, f32[1536]{0:T(1024)}, u32[]{:S(2)}) copy-start(f32[1536]{0:T(1024)} %param.24) | copy-start | bytes 18436
  85.5 91.1 %copy-start.6 = (s32[3072]{0:T(1024)S(1)}, s32[3072]{0:T(1024)}, u32[]{:S(2)}) copy-start(s32[3072]{0:T(1024)} %pad_clamp_fusion) | copy-start | bytes 36868
  174.3 1.2 copy-start.1
  176.6 17.9 %copy-start.7 = (pred[8,2,160]{2,1,0:T(4,128)(4,1)S(1)}, pred[8,2,160]{2,1,0:T(4,128)(4,1)}, u32[]{:S(2)}) copy-start(pred[8,2,160]{2,1,0:T(4,128)(4,1)} %broadcast_in_dim.101) | copy-start | bytes 7684
  200.6 3.6 collective-permute-start
  200.6 24.6 %collective-permute-start.1 = (bf16[1,2,160,1536]{3,2,1,0:T(8,128)(2,1)S(1)}, bf16[1,2,160,1536]{3,2,1,0:T(8,128)(2,1)S(1)}, u32[]{:S(2)}, u32[]{:S(2)}) collective-permute-start(bf16[1,2,160,1536]{3,2,1,0:T(8,128)(2,1)S(1)} %get-tuple-element.10), channel_id=1, source_target_pairs={{0,2},{1,3},{2,0},{3,1},{4,6},{5,7},{6,4},{7,5},{8,10},{9,11},{10,... | collective-permute-start | bytes 2949128 | tf_op jit(solution)/shard_map/ppermute | solution.py:137
  202.1 43.3 %collective-permute-start.2 = (bf16[1,2,160,1536]{3,2,1,0:T(8,128)(2,1)S(1)}, bf16[1,2,160,1536]{3,2,1,0:T(8,128)(2,1)S(1)}, u32[]{:S(2)}, u32[]{:S(2)}) collective-permute-start(bf16[1,2,160,1536]{3,2,1,0:T(8,128)(2,1)S(1)} %get-tuple-element.9), channel_id=1, source_target_pairs={{0,3},{1,2},{2,1},{3,0},{4,7},{5,6},{6,5},{7,4},{8,11},{9,10},{10,... | collective-permute-start | bytes 2949128 | tf_op jit(solution)/shard_map/ppermute | solution.py:137
  202.5 43.9 %collective-permute-start.3 = (bf16[1,2,160,1536]{3,2,1,0:T(8,128)(2,1)S(1)}, bf16[1,2,160,1536]{3,2,1,0:T(8,128)(2,1)S(1)}, u32[]{:S(2)}, u32[]{:S(2)}) collective-permute-start(bf16[1,2,160,1536]{3,2,1,0:T(8,128)(2,1)S(1)} %get-tuple-element.8), channel_id=1, source_target_pairs={{0,4},{1,5},{2,6},{3,7},{4,0},{5,1},{6,2},{7,3},{8,12},{9,13},{10,... | collective-permute-start | bytes 2949128 | tf_op jit(solution)/shard_map/ppermute | solution.py:137
  204.0 85.0 %collective-permute-start.4 = (bf16[1,2,160,1536]{3,2,1,0:T(8,128)(2,1)S(1)}, bf16[1,2,160,1536]{3,2,1,0:T(8,128)(2,1)S(1)}, u32[]{:S(2)}, u32[]{:S(2)}) collective-permute-start(bf16[1,2,160,1536]{3,2,1,0:T(8,128)(2,1)S(1)} %get-tuple-element.7), channel_id=1, source_target_pairs={{0,5},{1,4},{2,7},{3,6},{4,1},{5,0},{6,3},{7,2},{8,13},{9,12},{10,... | collective-permute-start | bytes 2949128 | tf_op jit(solution)/shard_map/ppermute | solution.py:137
  204.2 85.9 %collective-permute-start.5 = (bf16[1,2,160,1536]{3,2,1,0:T(8,128)(2,1)S(1)}, bf16[1,2,160,1536]{3,2,1,0:T(8,128)(2,1)S(1)}, u32[]{:S(2)}, u32[]{:S(2)}) collective-permute-start(bf16[1,2,160,1536]{3,2,1,0:T(8,128)(2,1)S(1)} %get-tuple-element.6), channel_id=1, source_target_pairs={{0,6},{1,7},{2,4},{3,5},{4,2},{5,3},{6,0},{7,1},{8,14},{9,15},{10,... | collective-permute-start | bytes 2949128 | tf_op jit(solution)/shard_map/ppermute | solution.py:137
  225.1 66.0 %collective-permute-start.6 = (bf16[1,2,160,1536]{3,2,1,0:T(8,128)(2,1)S(1)}, bf16[1,2,160,1536]{3,2,1,0:T(8,128)(2,1)S(1)}, u32[]{:S(2)}, u32[]{:S(2)}) collective-permute-start(bf16[1,2,160,1536]{3,2,1,0:T(8,128)(2,1)S(1)} %get-tuple-element.5), channel_id=1, source_target_pairs={{0,7},{1,6},{2,5},{3,4},{4,3},{5,2},{6,1},{7,0},{8,15},{9,14},{10,... | collective-permute-start | bytes 2949128 | tf_op jit(solution)/shard_map/ppermute | solution.py:137
  331.7 5.4 %copy-start.4 = (s32[256,8]{0,1:T(8,128)S(1)}, s32[256,8]{0,1:T(8,128)}, u32[]{:S(2)}) copy-start(s32[256,8]{0,1:T(8,128)} %param.26) | copy-start | bytes 24580
  331.7 5.6 %copy-start.5 = (f32[256,8]{0,1:T(8,128)S(1)}, f32[256,8]{0,1:T(8,128)}, u32[]{:S(2)}) copy-start(f32[256,8]{0,1:T(8,128)} %param.25) | copy-start | bytes 24580
  331.7 5.8 %copy-start.9 = (s32[2048,1]{0,1:T(1,128)S(1)}, s32[2048,1]{0,1:T(1,128)}, u32[]{:S(2)}) copy-start(s32[2048,1]{0,1:T(1,128)} %copy-done.8) | copy-start | bytes 24580
  331.7 93.6 %all-to-all-start = ((bf16[8,2,160,1536]{3,2,1,0:T(8,128)(2,1)}), bf16[8,2,160,1536]{3,2,1,0:T(8,128)(2,1)}, u32[]{:S(2)}, u32[]{:S(2)}) async-start(bf16[8,2,160,1536]{3,2,1,0:T(8,128)(2,1)} %copy.69), calls=%async_computation | async-start | bytes 15728640 | tf_op jit(solution)/shard_map/all_to_all | solution.py:140
  442.9 16.0 %copy-start.2 = (f32[256,1536]{1,0:T(8,128)S(1)}, f32[256,1536]{1,0:T(8,128)}, u32[]{:S(2)}) copy-start(f32[256,1536]{1,0:T(8,128)} %copy-done.1) | copy-start | bytes 4718596
Sparse Core Ops, SparseCore 0:
  9.2 35.0 all-gather.5
  46.2 32.3 all-gather.7
  80.1 89.4 all-gather.3
